TPU v7x, 32 devices: a whole 2x2x4 slice. The times are simulated.
32 devices in a mesh: expert: 8 (over y, x, core), tensor: 4 (over z).
Axes of the slice: x: 2, y: 2, z: 4, core: 2. Of those that a mesh axis runs over, the one named last changes fastest.
Arguments:
- tokens: bfloat16 [4096, 2560], P(('expert', 'tensor')), may hold values from -6 to 6
- expert_ids: int32 [4096, 1], P(('expert', 'tensor')), may hold values from 0 to 7; in each aligned block of 512 rows (0 to 511, 512 to 1023, ...) at most 128 rows name the same one
- gates: float32 [4096], P(('expert', 'tensor')), may hold values from 0.3 to 3
- w_gate: bfloat16 [8, 2560, 4096], P('expert', None, 'tensor'), may hold values from -0.125 to 0.125
- w_up: bfloat16 [8, 2560, 4096], P('expert', None, 'tensor'), may hold values from -0.125 to 0.125
- w_down: bfloat16 [8, 4096, 2560], P('expert', 'tensor'), may hold values from -0.09375 to 0.09375
- s_gate: bfloat16 [2560, 4096], P('expert', 'tensor'), may hold values from -0.125 to 0.125
- s_up: bfloat16 [2560, 4096], P('expert', 'tensor'), may hold values from -0.125 to 0.125
- s_down: bfloat16 [4096, 2560], P('tensor', 'expert'), may hold values from -0.09375 to 0.09375
Outputs:
- mixed: bfloat16 [4096, 2560], P(('expert', 'tensor'))
Inputs may be any that keep to these rules, and one draw needn't show every extreme that they name: `expert_ids`: in each aligned block of 512 tokens no expert is named by more than 128 tokens, and some block has an expert named by exactly 128 tokens.
All inputs are finite; a program needn't handle non-finite values.
Results may differ from a plain program's by a relative error of at most 0.013.
Values may be sent and summed in bfloat16 or wider, within the bound.
No kernel may reach another device: no remote copies, remote signals or barrier semaphores. Data moves between devices by JAX's collectives and lax.ppermute only.
A program may use at most 128 MiB of HBM per device.

v0:
```python
import jax
import jax.numpy as jnp
from jax import lax
from jax.sharding import PartitionSpec as P


def slots_of(ids, experts, cap):
    onehot = (ids[:, None] == jnp.arange(experts, dtype=jnp.int32)[None, :]).astype(jnp.int32)
    before = jnp.cumsum(onehot, axis=0) - onehot
    position = jnp.sum(before * onehot, axis=1)
    return ids * cap + position


def pick_rows(values, index):
    padded = jnp.concatenate([values, jnp.zeros((1, values.shape[1]), values.dtype)], axis=0)
    return jnp.take(padded, index, axis=0)


def body(tokens, expert_ids, gates, w_gate, w_up, w_down, s_gate, s_up, s_down):
    n_expert = lax.axis_size("expert")
    width = tokens.shape[1]
    group = lax.all_gather(tokens, "tensor", axis=0, tiled=True)
    group_ids = lax.all_gather(expert_ids, "tensor", axis=0, tiled=True)[:, 0]
    group_gates = lax.all_gather(gates, "tensor", axis=0, tiled=True)
    count = group.shape[0]
    experts = w_gate.shape[0] * n_expert
    cap = 2 * count // experts
    shared_gate = jnp.dot(
        group,
        lax.all_gather(s_gate, "expert", axis=0, tiled=True),
        preferred_element_type=jnp.float32,
    )
    shared_upper = jnp.dot(
        group,
        lax.all_gather(s_up, "expert", axis=0, tiled=True),
        preferred_element_type=jnp.float32,
    )
    shared_hidden = (jax.nn.silu(shared_gate) * shared_upper).astype(jnp.bfloat16)
    shared_part = jnp.dot(
        shared_hidden,
        lax.all_gather(s_down, "expert", axis=1, tiled=True),
        preferred_element_type=jnp.float32,
    )
    slot = slots_of(group_ids, experts, cap)
    owner = (
        jnp.full((experts * cap,), count, jnp.int32)
        .at[slot]
        .set(jnp.arange(count, dtype=jnp.int32))
    )
    outgoing = pick_rows(group, owner).reshape(experts, cap, width)
    received = lax.all_to_all(outgoing, "expert", split_axis=0, concat_axis=0, tiled=True)
    flat = received.reshape(-1, width)
    gate = jnp.dot(flat, w_gate[0], preferred_element_type=jnp.float32)
    upper = jnp.dot(flat, w_up[0], preferred_element_type=jnp.float32)
    hidden = (jax.nn.silu(gate) * upper).astype(jnp.bfloat16)
    result = jnp.dot(hidden, w_down[0], preferred_element_type=jnp.float32).astype(jnp.bfloat16)
    produced = result.reshape(received.shape[0], -1, width)
    returned = lax.all_to_all(produced, "expert", split_axis=0, concat_axis=0, tiled=True)
    routed_part = pick_rows(returned.reshape(experts * cap, width), slot).astype(jnp.float32)
    combined = (shared_part + group_gates[:, None] * routed_part).astype(jnp.bfloat16)
    return (
        lax.psum_scatter(combined, "tensor", scatter_dimension=0, tiled=True)
        .astype(jnp.float32)
        .astype(jnp.bfloat16)
    )


def solution(mesh):
    return jax.shard_map(
        body,
        mesh=mesh,
        in_specs=(
            P(("expert", "tensor"), None),
            P(("expert", "tensor"), None),
            P(("expert", "tensor")),
            P("expert", None, "tensor"),
            P("expert", None, "tensor"),
            P("expert", "tensor", None),
            P("expert", "tensor"),
            P("expert", "tensor"),
            P("tensor", "expert"),
        ),
        out_specs=P(("expert", "tensor"), None),
        check_vma=False,
    )
```

profile of v0, /device:TPU:0, one launch (start us, length us, event | category | flops | bytes accessed | tf_op | source)
XLA Modules:
  0.0 360.2 jit_solution(4594958189391389571)
XLA Ops:
  6.5 0.0 all-gather.6.cloned.1.call-start
  6.5 0.7 all-gather.6.cloned.1.call-update
  7.3 0.0 all-gather.8.cloned.1.call-start
  7.3 0.7 all-gather.8.cloned.1.call-update
  8.0 0.0 all-gather.10.cloned.1.call-start
  8.1 0.7 all-gather.10.cloned.1.call-update
  8.7 12.8 %all_gather.23 = s32[512,1]{0,1:T(1,128)S(1)} all-gather(s32[128,1]{0,1:T(1,128)} %param.10), channel_id=1, replica_groups=mesh['expert'=8,'tensor'=4] {'tensor'}, dimensions={0}, use_global_device_ids=true | all-gather | bytes 2560 | tf_op jit(solution)/shard_map/all_gather | solution.py:23
  21.5 1.1 reduce-window.6
  22.7 0.2 slice_reduce_fusion
  22.9 0.1 fusion.10
  23.1 2.4 scatter_custom_fusion
  25.5 40.9 %all-gather.6.cloned.1.call-done = bf16[512,2560]{1,0:T(8,128)(2,1)} async-done(((bf16[128,2560]{1,0:T(8,128)(2,1)}), bf16[512,2560]{1,0:T(8,128)(2,1)}) %all-gather.6.cloned.1.call-update) | async-done | bytes 2621456 | tf_op jit(solution)/shard_map/all_gather | solution.py:22
  66.4 1.9 concatenate.6
  68.3 6.4 %gather_fusion = bf16[1024,2560]{1,0:T(8,128)(2,1)} fusion(bf16[513,2560]{1,0:T(8,128)(2,1)S(1)} %concatenate.6, s32[1024]{0:T(1024)S(1)} %fusion.12), kind=kCustom, calls=%fused_computation | custom fusion | bytes 10489856 | tf_op jit(solution)/shard_map/jit(_take)/gather | solution.py:16
  74.7 5.5 %broadcast_select_fusion = bf16[8,128,2560]{2,1,0:T(8,128)(2,1)} fusion(bf16[8,128,2560]{2,1,0:T(8,128)(2,1)} %bitcast.41, pred[8,128]{1,0:T(8,128)(4,1)S(1)} %and_bitcast_fusion), kind=kLoop, calls=%fused_computation.10 | loop fusion | flops 2621440 | bytes 10486784 | tf_op jit(solution)/shard_map/jit(_take)/select_n | solution.py:16
  80.2 4.6 %all-to-all-start = ((bf16[8,128,2560]{2,1,0:T(8,128)(2,1)}), bf16[8,128,2560]{2,1,0:T(8,128)(2,1)}, u32[]{:S(2)}, u32[]{:S(2)}) async-start(bf16[8,128,2560]{2,1,0:T(8,128)(2,1)} %broadcast_select_fusion), calls=%async_computation | async-start | bytes 10485760 | tf_op jit(solution)/shard_map/all_to_all | solution.py:51
  84.8 0.0 all-gather.12.cloned.1.call-start
  84.9 0.5 all-gather.12.cloned.1.call-update
  85.4 80.8 %all-to-all-done = bf16[8,128,2560]{2,1,0:T(8,128)(2,1)} async-done(((bf16[8,128,2560]{2,1,0:T(8,128)(2,1)}), bf16[8,128,2560]{2,1,0:T(8,128)(2,1)}, u32[]{:S(2)}, u32[]{:S(2)}) %all-to-all-start) | async-done | bytes 5242912 | tf_op jit(solution)/shard_map/all_to_all | solution.py:51
  166.2 11.2 %fusion.1 = f32[1024,1024]{1,0:T(8,128)} fusion(bf16[1024,2560]{1,0:T(8,128)(2,1)} %bitcast.10, bf16[1,2560,1024]{2,1,0:T(8,128)(2,1)} %param.13), kind=kOutput, calls=%fused_computation.5 | convolution fusion | flops 5368709120 | bytes 14680064 | tf_op jit(solution)/shard_map/dot_general | solution.py:54
  177.4 18.6 %convolution_convert_fusion = bf16[1024,2560]{1,0:T(8,128)(2,1)} fusion(bf16[1,1024,2560]{2,1,0:T(8,128)(2,1)} %param.14, f32[1024,1024]{1,0:T(8,128)} %fusion.1, bf16[1024,2560]{1,0:T(8,128)(2,1)} %bitcast.10, bf16[1,2560,1024]{2,1,0:T(8,128)(2,1)} %param.12), kind=kOutput, calls=%fused_computation.3 | convolution fusion | flops 10746331136 | bytes 25165824 | tf_op jit(solution)/shard_map/dot_general | solution.py:56
  196.0 0.0 copy-start.1
  196.0 0.0 copy-start
  196.0 4.9 %all-to-all-start.1 = ((bf16[8,128,2560]{2,1,0:T(8,128)(2,1)}), bf16[8,128,2560]{2,1,0:T(8,128)(2,1)}, u32[]{:S(2)}, u32[]{:S(2)}) async-start(bf16[8,128,2560]{2,1,0:T(8,128)(2,1)} %bitcast.42), calls=%async_computation.1 | async-start | bytes 10485760 | tf_op jit(solution)/shard_map/all_to_all | solution.py:58
  200.9 0.0 reduce-scatter.2.cloned.1.call-start
  200.9 0.0 copy-done.1
  201.0 7.8 %all-gather = f32[4,1,128]{2,1,0:T(1,128)S(1)} all-gather(f32[1,1,128]{2,1,0:T(1,128)S(1)} %bitcast.50), channel_id=1, replica_groups=mesh['expert'=8,'tensor'=4] {'tensor'}, dimensions={0}, use_global_device_ids=true | all-gather | bytes 2560 | tf_op jit(solution)/shard_map/all_gather | solution.py:24
  208.8 0.0 all-gather.8.cloned.1.call-done
  208.8 0.0 copy-done
  208.9 6.7 %fusion.17 = f32[512,1024]{1,0:T(8,128)} fusion(bf16[512,2560]{1,0:T(8,128)(2,1)S(1)} %copy-done, bf16[2560,1024]{1,0:T(8,128)(2,1)} %all-gather.8.cloned.1.call-done), kind=kOutput, calls=%fused_computation.32 | convolution fusion | flops 2684354560 | bytes 9961472 | tf_op jit(solution)/shard_map/dot_general | solution.py:28
  215.5 60.2 %all-to-all-done.1 = bf16[8,128,2560]{2,1,0:T(8,128)(2,1)} async-done(((bf16[8,128,2560]{2,1,0:T(8,128)(2,1)}), bf16[8,128,2560]{2,1,0:T(8,128)(2,1)}, u32[]{:S(2)}, u32[]{:S(2)}) %all-to-all-start.1) | async-done | bytes 5242912 | tf_op jit(solution)/shard_map/all_to_all | solution.py:58
  275.7 5.1 %concatenate.7 = bf16[1025,2560]{1,0:T(8,128)(2,1)} pad(bf16[1024,2560]{1,0:T(8,128)(2,1)} %bitcast.15, bf16[]{:T(256)} %constant.45.clone.1), padding=0_1x0_0 | pad | bytes 10490882 | tf_op jit(solution)/shard_map/concatenate | solution.py:15
  280.8 8.4 %gather_fusion.1 = bf16[512,2560]{1,0:T(8,128)(2,1)S(1)} fusion(bf16[1025,2560]{1,0:T(8,128)(2,1)} %concatenate.7, s32[1024]{0:T(1024)S(1)} %pad_clamp_fusion), kind=kCustom, calls=%fused_computation.1 | custom fusion | bytes 5244928 | tf_op jit(solution)/shard_map/jit(_take)/gather | solution.py:16
  289.2 0.0 all-gather.10.cloned.1.call-done
  289.2 0.0 all-gather.12.cloned.1.call-done
  289.3 12.6 %add_convert_fusion = bf16[512,2560]{1,0:T(8,128)(2,1)} fusion(bf16[1024,2560]{0,1:T(8,128)(2,1)} %all-gather.12.cloned.1.call-done, bf16[512,2560]{1,0:T(8,128)(2,1)S(1)} %gather_fusion.1, f32[512]{0:T(512)S(1)} %bitcast.49, pred[512]{0:T(512)(128)(4,1)S(1)} %get-tuple-element.5, f32[512,1024]{1,0:T(8,128)} %fusion.17, ...), kind=kOutput, calls=%fused_computation.9 | convolution fusion | flops 5378408448 | bytes 20449792 | tf_op jit(solution)/shard_map/dot_general | solution.py:39
  301.9 0.0 reduce-scatter.2.cloned.1.call-update
  301.9 51.8 %reduce-scatter.2.cloned.1.call-done = bf16[128,2560]{1,0:T(8,128)(2,1)} async-done(((bf16[512,2560]{1,0:T(8,128)(2,1)}), bf16[128,2560]{1,0:T(8,128)(2,1)}) %reduce-scatter.2.cloned.1.call-update) | async-done | bytes 655376 | tf_op jit(solution)/shard_map/reduce_scatter | solution.py:62
  (9 shorter events, 0.1 us)
Async XLA Ops:
  6.5 59.9 %all-gather.6.cloned.1.call-start = ((), (), s32[]{:S(2)}) async-start(), calls=%async_computation.3 | async-start | bytes 3276800 | tf_op jit(solution)/shard_map/all_gather | solution.py:22
  7.3 201.6 %all-gather.8.cloned.1.call-start = ((), (), s32[]{:S(2)}) async-start(), calls=%async_computation.4 | async-start | bytes 5898240 | tf_op jit(solution)/shard_map/all_gather | solution.py:30
  8.0 281.2 %all-gather.10.cloned.1.call-start = ((), (), s32[]{:S(2)}) async-start(), calls=%async_computation.5 | async-start | bytes 5898240 | tf_op jit(solution)/shard_map/all_gather | solution.py:35
  80.2 86.0 %all-to-all-start = ((bf16[8,128,2560]{2,1,0:T(8,128)(2,1)}), bf16[8,128,2560]{2,1,0:T(8,128)(2,1)}, u32[]{:S(2)}, u32[]{:S(2)}) async-start(bf16[8,128,2560]{2,1,0:T(8,128)(2,1)} %broadcast_select_fusion), calls=%async_computation | async-start | bytes 10485760 | tf_op jit(solution)/shard_map/all_to_all | solution.py:51
  84.8 204.4 %all-gather.12.cloned.1.call-start = ((), (), s32[]{:S(2)}) async-start(), calls=%async_computation.6 | async-start | bytes 5898240 | tf_op jit(solution)/shard_map/all_gather | solution.py:41
  196.0 5.0 %copy-start.1 = (f32[128]{0:T(128)S(1)}, f32[128]{0:T(128)}, u32[]{:S(2)}) copy-start(f32[128]{0:T(128)} %param.11) | copy-start | bytes 1540
  196.0 12.9 %copy-start = (bf16[512,2560]{1,0:T(8,128)(2,1)S(1)}, bf16[512,2560]{1,0:T(8,128)(2,1)}, u32[]{:S(2)}) copy-start(bf16[512,2560]{1,0:T(8,128)(2,1)} %all-gather.6.cloned.1.call-done) | copy-start | bytes 7864324
  196.0 79.7 %all-to-all-start.1 = ((bf16[8,128,2560]{2,1,0:T(8,128)(2,1)}), bf16[8,128,2560]{2,1,0:T(8,128)(2,1)}, u32[]{:S(2)}, u32[]{:S(2)}) async-start(bf16[8,128,2560]{2,1,0:T(8,128)(2,1)} %bitcast.42), calls=%async_computation.1 | async-start | bytes 10485760 | tf_op jit(solution)/shard_map/all_to_all | solution.py:58
  200.9 152.8 %reduce-scatter.2.cloned.1.call-start = ((), (), s32[]{:S(2)}) async-start(), calls=%async_computation.7 | async-start | bytes 3276800 | tf_op jit(solution)/shard_map/reduce_scatter | solution.py:62
Sparse Core Ops, SparseCore 0:
  8.9 57.4 all-gather.5
  68.3 67.9 all-gather.7
  138.1 47.1 all-gather.9
  187.1 75.5 all-gather.11
  302.0 51.6 reduce-scatter.1
where the time goes:
time: 361 us; the launch traced here: 360 us
  waiting for transfers between devices  236 us (65%)
  matrix products  49.1 us (14%)
  local copies, waits for them, and re-layouts  24.5 us (7%)
  blocking collectives  20.6 us (6%)
  between operations  13.3 us (4%)
  starting transfers between devices  9.71 us (3%)
  other arithmetic  6.81 us (2%)
    all_to_all x1, waiting for transfers between devices, body(): lax.all_to_all(outgoing, 'expert', split_axis=0, concat_axis=0, tiled=True)  80.8 us
    all_to_all x1, waiting for transfers between devices, body(): lax.all_to_all(produced, 'expert', split_axis=0, concat_axis=0, tiled=True)  60.2 us
    reduce_scatter x1, waiting for transfers between devices, body(): lax.psum_scatter(combined, 'tensor', scatter_dimension=0, tiled=True)  51.8 us
    all_gather x1, waiting for transfers between devices, body(): group = lax.all_gather(tokens, 'tensor', axis=0, tiled=True)  40.9 us
    dot_general x1, matrix products, body(): jnp.dot(hidden, w_down[0], preferred_element_type=jnp.float32)  18.6 us
    gather x2, local copies, waits for them, and re-layouts, pick_rows(): return jnp.take(padded, index, axis=0)  14.7 us
    all_gather x1, blocking collectives, body(): group_ids = lax.all_gather(expert_ids, 'tensor', axis=0, tiled=True)[:, 0]  12.8 us
    dot_general x1, matrix products, body(): jnp.dot(shared_hidden, lax.all_gather(s_down, 'expert', axis=1, tiled=Tru...  12.6 us
  transfers between devices with their start and end apart: 7, of which 4 were waited for; matrix products, arithmetic and copies ran while one was open for 19% of the time, Pallas kernels for 0%

commit v1 on v0

--- a/solution.py
+++ b/solution.py
@@ -19,7 +19,14 @@
 def body(tokens, expert_ids, gates, w_gate, w_up, w_down, s_gate, s_up, s_down):
     n_expert = lax.axis_size("expert")
     width = tokens.shape[1]
-    group = lax.all_gather(tokens, "tensor", axis=0, tiled=True)
+    ring = [tokens]
+    for hop in range(3):
+        ring.append(lax.ppermute(ring[-1], "tensor", [(dev, (dev + 1) % 4) for dev in range(4)]))
+    group = jnp.roll(
+        jnp.concatenate(ring[::-1], axis=0),
+        (lax.axis_index("tensor") + 1) * ring[0].shape[0],
+        axis=0,
+    )
     group_ids = lax.all_gather(expert_ids, "tensor", axis=0, tiled=True)[:, 0]
     group_gates = lax.all_gather(gates, "tensor", axis=0, tiled=True)
     count = group.shape[0]

time: 361 us -> 338 us (0.936)
  waiting for transfers between devices: 236 us -> 198 us
  blocking collectives: 20.6 us -> 30.6 us
  starting transfers between devices: 9.71 us -> 14.7 us
    all_gather x1 -> x0, waiting for transfers between devices: 40.9 us -> none  [body(): group = lax.all_gather(tokens, 'tensor', axis=0, tiled=True)]
    ppermute x0 -> x3, waiting for transfers between devices: none -> 28.9 us  [body(): lax.ppermute(ring[-1], 'tensor', [(dev, (dev + 1) % 4) for dev in range(4)])]
    all_to_all x1, waiting for transfers between devices: 60.2 us -> 42.5 us  [body(): lax.all_to_all(produced, 'expert', split_axis=0, concat_axis=0, tiled=True)]
    all_to_all x1, waiting for transfers between devices: 80.8 us -> 74 us  [body(): lax.all_to_all(outgoing, 'expert', split_axis=0, concat_axis=0, tiled=True)]
    all_gather x1, blocking collectives: 12.8 us -> 19.5 us  [body(): group_ids = lax.all_gather(expert_ids, 'tensor', axis=0, tiled=True)[:, 0]]
    ppermute x0 -> x3, starting transfers between devices: none -> 4.99 us  [body(): lax.ppermute(ring[-1], 'tensor', [(dev, (dev + 1) % 4) for dev in range(4)])]
  transfers between devices with their start and end apart: 7 -> 9, of which waited for: 4 -> 5; matrix products, arithmetic and copies ran while one was open for 19% -> 20% of each run, Pallas kernels for 0% -> 0%
where the time goes in v1:
time: 338 us
  waiting for transfers between devices  198 us (59%)
  matrix products  48.4 us (14%)
  blocking collectives  30.6 us (9%)
  local copies, waits for them, and re-layouts  25.7 us (8%)
  starting transfers between devices  14.7 us (4%)
  between operations  13.3 us (4%)
  other arithmetic  6.96 us (2%)
    all_to_all x1, waiting for transfers between devices, body(): lax.all_to_all(outgoing, 'expert', split_axis=0, concat_axis=0, tiled=True)  74 us
    reduce_scatter x1, waiting for transfers between devices, body(): lax.psum_scatter(combined, 'tensor', scatter_dimension=0, tiled=True)  51.5 us
    all_to_all x1, waiting for transfers between devices, body(): lax.all_to_all(produced, 'expert', split_axis=0, concat_axis=0, tiled=True)  42.5 us
    ppermute x3, waiting for transfers between devices, body(): lax.ppermute(ring[-1], 'tensor', [(dev, (dev + 1) % 4) for dev in range(4)])  28.9 us
    all_gather x1, blocking collectives, body(): group_ids = lax.all_gather(expert_ids, 'tensor', axis=0, tiled=True)[:, 0]  19.5 us
    dot_general x1, matrix products, body(): jnp.dot(hidden, w_down[0], preferred_element_type=jnp.float32)  18.7 us
    gather x2, local copies, waits for them, and re-layouts, pick_rows(): return jnp.take(padded, index, axis=0)  15.7 us
    dot_general x1, matrix products, body(): jnp.dot(shared_hidden, lax.all_gather(s_down, 'expert', axis=1, tiled=Tru...  12.6 us
  transfers between devices with their start and end apart: 9, of which 5 were waited for; matrix products, arithmetic and copies ran while one was open for 20% of the time, Pallas kernels for 0%

profile of v1, /device:TPU:0, one launch (start us, length us, event | category | flops | bytes accessed | tf_op | source)
XLA Modules:
  0.0 338.0 jit_solution(16108350416693370953)
XLA Ops:
  6.5 0.0 copy-start.2
  6.5 0.0 all-gather.5.cloned.1.call-start
  6.5 0.7 all-gather.5.cloned.1.call-update
  7.3 0.0 all-gather.7.cloned.1.call-start
  7.3 3.1 collective-permute-start
  10.4 17.0 %collective-permute-done = bf16[128,2560]{1,0:T(8,128)(2,1)S(1)} collective-permute-done((bf16[128,2560]{1,0:T(8,128)(2,1)}, bf16[128,2560]{1,0:T(8,128)(2,1)S(1)}, u32[]{:S(2)}, u32[]{:S(2)}) %collective-permute-start) | collective-permute-done | bytes 655392 | tf_op jit(solution)/shard_map/ppermute | solution.py:24
  27.4 0.0 collective-permute-start.1
  27.4 0.0 all-gather.7.cloned.1.call-update
  27.4 19.5 %all_gather.19 = s32[512,1]{0,1:T(1,128)S(1)} all-gather(s32[128,1]{0,1:T(1,128)} %param.10), channel_id=1, replica_groups=mesh['expert'=8,'tensor'=4] {'tensor'}, dimensions={0}, use_global_device_ids=true | all-gather | bytes 2560 | tf_op jit(solution)/shard_map/all_gather | solution.py:30
  46.9 1.1 reduce-window.6
  48.1 0.2 slice_reduce_fusion
  48.3 0.1 fusion.11
  48.4 0.0 collective-permute-done.1
  48.4 1.9 collective-permute-start.2
  50.3 2.4 scatter_custom_fusion
  52.8 11.9 %collective-permute-done.2 = bf16[128,2560]{1,0:T(8,128)(2,1)S(1)} collective-permute-done((bf16[128,2560]{1,0:T(8,128)(2,1)S(1)}, bf16[128,2560]{1,0:T(8,128)(2,1)S(1)}, u32[]{:S(2)}, u32[]{:S(2)}) %collective-permute-start.2) | collective-permute-done | bytes 655392 | tf_op jit(solution)/shard_map/ppermute | solution.py:24
  64.9 0.0 copy-done.2
  65.2 0.2 constant_dynamic-slice_fusion
  65.3 0.0 copy-start
  65.4 1.5 copy-done
  66.8 0.2 concatenate.13
  67.0 6.3 %gather_fusion = bf16[1024,2560]{1,0:T(8,128)(2,1)} fusion(bf16[513,2560]{1,0:T(8,128)(2,1)S(1)} %concatenate.13, s32[1024]{0:T(1024)S(1)} %fusion.13), kind=kCustom, calls=%fused_computation | custom fusion | bytes 10489856 | tf_op jit(solution)/shard_map/jit(_take)/gather | solution.py:16
  73.3 5.6 %broadcast_select_fusion = bf16[8,128,2560]{2,1,0:T(8,128)(2,1)} fusion(bf16[8,128,2560]{2,1,0:T(8,128)(2,1)} %bitcast.41, pred[8,128]{1,0:T(8,128)(4,1)S(1)} %and_bitcast_fusion), kind=kLoop, calls=%fused_computation.10 | loop fusion | flops 2621440 | bytes 10486784 | tf_op jit(solution)/shard_map/jit(_take)/select_n | solution.py:16
  79.0 4.6 %all-to-all-start = ((bf16[8,128,2560]{2,1,0:T(8,128)(2,1)}), bf16[8,128,2560]{2,1,0:T(8,128)(2,1)}, u32[]{:S(2)}, u32[]{:S(2)}) async-start(bf16[8,128,2560]{2,1,0:T(8,128)(2,1)} %broadcast_select_fusion), calls=%async_computation | async-start | bytes 10485760 | tf_op jit(solution)/shard_map/all_to_all | solution.py:58
  83.6 0.0 all-gather.9.cloned.1.call-start
  83.7 0.7 all-gather.9.cloned.1.call-update
  84.4 74.0 %all-to-all-done = bf16[8,128,2560]{2,1,0:T(8,128)(2,1)} async-done(((bf16[8,128,2560]{2,1,0:T(8,128)(2,1)}), bf16[8,128,2560]{2,1,0:T(8,128)(2,1)}, u32[]{:S(2)}, u32[]{:S(2)}) %all-to-all-start) | async-done | bytes 5242912 | tf_op jit(solution)/shard_map/all_to_all | solution.py:58
  158.4 10.4 %fusion.1 = f32[1024,1024]{1,0:T(8,128)} fusion(bf16[1024,2560]{1,0:T(8,128)(2,1)} %bitcast.10, bf16[1,2560,1024]{2,1,0:T(8,128)(2,1)} %param.13), kind=kOutput, calls=%fused_computation.5 | convolution fusion | flops 5368709120 | bytes 14680064 | tf_op jit(solution)/shard_map/dot_general | solution.py:61
  168.8 18.7 %convolution_convert_fusion = bf16[1024,2560]{1,0:T(8,128)(2,1)} fusion(bf16[1,1024,2560]{2,1,0:T(8,128)(2,1)} %param.14, f32[1024,1024]{1,0:T(8,128)} %fusion.1, bf16[1024,2560]{1,0:T(8,128)(2,1)} %bitcast.10, bf16[1,2560,1024]{2,1,0:T(8,128)(2,1)} %param.12), kind=kOutput, calls=%fused_computation.3 | convolution fusion | flops 10746331136 | bytes 25165824 | tf_op jit(solution)/shard_map/dot_general | solution.py:63
  187.5 0.0 copy-start.3
  187.5 0.0 copy-start.1
  187.5 4.9 %all-to-all-start.1 = ((bf16[8,128,2560]{2,1,0:T(8,128)(2,1)}), bf16[8,128,2560]{2,1,0:T(8,128)(2,1)}, u32[]{:S(2)}, u32[]{:S(2)}) async-start(bf16[8,128,2560]{2,1,0:T(8,128)(2,1)} %bitcast.42), calls=%async_computation.1 | async-start | bytes 10485760 | tf_op jit(solution)/shard_map/all_to_all | solution.py:65
  192.5 0.0 reduce-scatter.2.cloned.1.call-start
  192.5 0.0 copy-done.3
  192.5 11.1 %all-gather = f32[4,1,128]{2,1,0:T(1,128)S(1)} all-gather(f32[1,1,128]{2,1,0:T(1,128)S(1)} %bitcast.50), channel_id=1, replica_groups=mesh['expert'=8,'tensor'=4] {'tensor'}, dimensions={0}, use_global_device_ids=true | all-gather | bytes 2560 | tf_op jit(solution)/shard_map/all_gather | solution.py:31
  203.6 0.0 all-gather.5.cloned.1.call-done
  203.7 0.0 copy-done.1
  203.7 6.6 %fusion.20 = f32[512,1024]{1,0:T(8,128)} fusion(bf16[512,2560]{1,0:T(8,128)(2,1)S(1)} %copy-done.1, bf16[2560,1024]{1,0:T(8,128)(2,1)} %all-gather.5.cloned.1.call-done), kind=kOutput, calls=%fused_computation.43 | convolution fusion | flops 2684354560 | bytes 9961472 | tf_op jit(solution)/shard_map/dot_general | solution.py:35
  210.3 42.5 %all-to-all-done.1 = bf16[8,128,2560]{2,1,0:T(8,128)(2,1)} async-done(((bf16[8,128,2560]{2,1,0:T(8,128)(2,1)}), bf16[8,128,2560]{2,1,0:T(8,128)(2,1)}, u32[]{:S(2)}, u32[]{:S(2)}) %all-to-all-start.1) | async-done | bytes 5242912 | tf_op jit(solution)/shard_map/all_to_all | solution.py:65
  252.8 5.2 %concatenate.14 = bf16[1025,2560]{1,0:T(8,128)(2,1)} pad(bf16[1024,2560]{1,0:T(8,128)(2,1)} %bitcast.15, bf16[]{:T(256)} %constant.72.clone.1), padding=0_1x0_0 | pad | bytes 10490882 | tf_op jit(solution)/shard_map/concatenate | solution.py:15
  258.0 9.3 %gather_fusion.1 = bf16[512,2560]{1,0:T(8,128)(2,1)} fusion(bf16[1025,2560]{1,0:T(8,128)(2,1)} %concatenate.14, s32[1024]{0:T(1024)S(1)} %pad_clamp_fusion), kind=kCustom, calls=%fused_computation.1 | custom fusion | bytes 5244928 | tf_op jit(solution)/shard_map/jit(_take)/gather | solution.py:16
  267.3 0.0 all-gather.7.cloned.1.call-done
  267.3 0.0 all-gather.9.cloned.1.call-done
  267.3 12.6 %add_convert_fusion = bf16[512,2560]{1,0:T(8,128)(2,1)} fusion(bf16[1024,2560]{0,1:T(8,128)(2,1)} %all-gather.9.cloned.1.call-done, bf16[512,2560]{1,0:T(8,128)(2,1)} %gather_fusion.1, f32[512]{0:T(512)S(1)} %bitcast.49, pred[512]{0:T(512)(128)(4,1)S(1)} %get-tuple-element.5, f32[512,1024]{1,0:T(8,128)} %fusion.20, bf16[512,2560]{1,0:T(8,128)(2,1)S(1)} %copy-done.1, ...), kind=kOutput, calls=%fused_computation.9 | convolution fusion | flops 5378408448 | bytes 20449792 | tf_op jit(solution)/shard_map/dot_general | solution.py:46
  279.9 0.0 reduce-scatter.2.cloned.1.call-update
  279.9 51.5 %reduce-scatter.2.cloned.1.call-done = bf16[128,2560]{1,0:T(8,128)(2,1)} async-done(((bf16[512,2560]{1,0:T(8,128)(2,1)}), bf16[128,2560]{1,0:T(8,128)(2,1)}) %reduce-scatter.2.cloned.1.call-update) | async-done | bytes 655376 | tf_op jit(solution)/shard_map/reduce_scatter | solution.py:69
  (17 shorter events, 0.5 us)
Async XLA Ops:
  6.5 58.4 %copy-start.2 = (bf16[128,2560]{1,0:T(8,128)(2,1)S(1)}, bf16[128,2560]{1,0:T(8,128)(2,1)}, u32[]{:S(2)}) copy-start(bf16[128,2560]{1,0:T(8,128)(2,1)} %param.9) | copy-start | bytes 1966084
  6.5 197.1 %all-gather.5.cloned.1.call-start = ((), (), s32[]{:S(2)}) async-start(), calls=%async_computation.3 | async-start | bytes 5898240 | tf_op jit(solution)/shard_map/all_gather | solution.py:37
  7.3 260.0 %all-gather.7.cloned.1.call-start = ((), (), s32[]{:S(2)}) async-start(), calls=%async_computation.4 | async-start | bytes 5898240 | tf_op jit(solution)/shard_map/all_gather | solution.py:42
  7.3 20.1 %collective-permute-start = (bf16[128,2560]{1,0:T(8,128)(2,1)}, bf16[128,2560]{1,0:T(8,128)(2,1)S(1)}, u32[]{:S(2)}, u32[]{:S(2)}) collective-permute-start(bf16[128,2560]{1,0:T(8,128)(2,1)} %param.9), channel_id=1, source_target_pairs={{0,1},{1,2},{2,3},{3,0},{4,5},{5,6},{6,7},{7,4},{8,9},{9,10},{10,1... | collective-permute-start | bytes 1966088 | tf_op jit(solution)/shard_map/ppermute | solution.py:24
  27.4 21.0 %collective-permute-start.1 = (bf16[128,2560]{1,0:T(8,128)(2,1)S(1)}, bf16[128,2560]{1,0:T(8,128)(2,1)S(1)}, u32[]{:S(2)}, u32[]{:S(2)}) collective-permute-start(bf16[128,2560]{1,0:T(8,128)(2,1)S(1)} %collective-permute-done), channel_id=1, source_target_pairs={{0,1},{1,2},{2,3},{3,0},{4,5},{5,6},{6,7},{7,4},{8,9},{9,10},{10,1... | collective-permute-start | bytes 1966088 | tf_op jit(solution)/shard_map/ppermute | solution.py:24
  48.4 16.3 %collective-permute-start.2 = (bf16[128,2560]{1,0:T(8,128)(2,1)S(1)}, bf16[128,2560]{1,0:T(8,128)(2,1)S(1)}, u32[]{:S(2)}, u32[]{:S(2)}) collective-permute-start(bf16[128,2560]{1,0:T(8,128)(2,1)S(1)} %collective-permute-done.1), channel_id=1, source_target_pairs={{0,1},{1,2},{2,3},{3,0},{4,5},{5,6},{6,7},{7,4},{8,9},{9,10},{10,1... | collective-permute-start | bytes 1966088 | tf_op jit(solution)/shard_map/ppermute | solution.py:24
  65.3 1.5 copy-start
  79.0 79.4 %all-to-all-start = ((bf16[8,128,2560]{2,1,0:T(8,128)(2,1)}), bf16[8,128,2560]{2,1,0:T(8,128)(2,1)}, u32[]{:S(2)}, u32[]{:S(2)}) async-start(bf16[8,128,2560]{2,1,0:T(8,128)(2,1)} %broadcast_select_fusion), calls=%async_computation | async-start | bytes 10485760 | tf_op jit(solution)/shard_map/all_to_all | solution.py:58
  83.6 183.7 %all-gather.9.cloned.1.call-start = ((), (), s32[]{:S(2)}) async-start(), calls=%async_computation.5 | async-start | bytes 5898240 | tf_op jit(solution)/shard_map/all_gather | solution.py:48
  187.5 5.0 %copy-start.3 = (f32[128]{0:T(128)S(1)}, f32[128]{0:T(128)}, u32[]{:S(2)}) copy-start(f32[128]{0:T(128)} %param.11) | copy-start | bytes 1540
  187.5 16.1 %copy-start.1 = (bf16[512,2560]{1,0:T(8,128)(2,1)S(1)}, bf16[512,2560]{1,0:T(8,128)(2,1)}, u32[]{:S(2)}) copy-start(bf16[512,2560]{1,0:T(8,128)(2,1)} %copy-done) | copy-start | bytes 7864324
  187.5 65.3 %all-to-all-start.1 = ((bf16[8,128,2560]{2,1,0:T(8,128)(2,1)}), bf16[8,128,2560]{2,1,0:T(8,128)(2,1)}, u32[]{:S(2)}, u32[]{:S(2)}) async-start(bf16[8,128,2560]{2,1,0:T(8,128)(2,1)} %bitcast.42), calls=%async_computation.1 | async-start | bytes 10485760 | tf_op jit(solution)/shard_map/all_to_all | solution.py:65
  192.5 139.0 %reduce-scatter.2.cloned.1.call-start = ((), (), s32[]{:S(2)}) async-start(), calls=%async_computation.6 | async-start | bytes 3276800 | tf_op jit(solution)/shard_map/reduce_scatter | solution.py:69
Sparse Core Ops, SparseCore 0:
  9.2 43.6 all-gather.4
  54.8 48.3 all-gather.6
  105.2 68.8 all-gather.8
  280.0 51.3 reduce-scatter.1
